TPU v7x, 128 devices: a whole 4x4x4 slice. The times are simulated.
128 devices in a mesh: section: 2 (over x_hi), seq: 16 (over z, y), mp: 4 (over x_lo, core).
Axes of the slice: x: 4 (x_hi: 2, x_lo: 2; x = x_hi * 2 + x_lo), y: 4, z: 4, core: 2. Of those that a mesh axis runs over, the one named last changes fastest.
Arguments:
- video: bfloat16 [2, 4, 128, 3072], P(None, None, 'seq'), may hold values from -6 to 6
- text: bfloat16 [2, 128, 3072], P(None, 'seq'), may hold values from -6 to 6
- patch_lengths: int32 [2, 4], replicated, may hold values from 1 to 128, 384 in all within a row
- text_len: int32 [2], replicated, may hold values from 64 to 128, as said below
- timestep: int32 [1], replicated, may hold values from 0 to 999
- w_mod: bfloat16 [2, 512, 9216], P('section', None, 'mp'), may hold values from -0.25 to 0.25
- w_qkv: bfloat16 [2, 3072, 3, 3072], P('section', None, None, 'mp')
- w_out: bfloat16 [2, 3072, 3072], P('section', 'mp'), may hold values from -0.109375 to 0.109375
- stale_cache: bfloat16 [2, 2, 4, 128, 2, 3072], P('section', None, None, 'seq', None, 'mp'), may hold values from -6 to 6
Outputs:
- hidden_video: bfloat16 [2, 2, 4, 128, 3072], P('section', None, None, 'seq')
- hidden_text: bfloat16 [2, 2, 128, 3072], P('section', None, 'seq')
- cache_video: bfloat16 [2, 2, 4, 128, 2, 3072], P('section', None, None, 'seq', None, 'mp')
- cache_text: bfloat16 [2, 2, 128, 2, 3072], P('section', None, 'seq', None, 'mp')
Inputs may be any that keep to these rules, and one draw needn't show every extreme that they name: `patch_lengths`: 4 patch lengths per request summing to 384; in every request the largest is 128. `text_len`: exactly one request has 128, every other fewer.
All inputs are finite; a program needn't handle non-finite values.
Results may differ from a plain program's by a relative error of at most 0.01.
Values may be sent and summed in bfloat16 or wider, within the bound.
No kernel may reach another device: no remote copies, remote signals or barrier semaphores. Data moves between devices by JAX's collectives and lax.ppermute only.
A program may use at most 192 MiB of HBM per device.

v0:
```python
import math
import jax
import jax.numpy as jnp
from jax import lax
from jax.sharding import PartitionSpec as P

HEAD = 64
EPS = 1e-05
NEG = -1e30


def passed_along(value, axis, steps):
    count = lax.axis_size(axis)
    leading, last = (max(0, -steps), min(count, count - steps))
    return lax.ppermute(value, axis, [(source, source + steps) for source in range(leading, last)])


def modulation(timestep, weight):
    half_width = weight.shape[0] // 2
    frequency = jnp.exp(-math.log(10000.0) * jnp.arange(half_width, dtype=jnp.float32) / half_width)
    phases = timestep.astype(jnp.float32)[0] * frequency
    embedding = jnp.concatenate([jnp.cos(phases), jnp.sin(phases)])
    active = jax.nn.silu(embedding).astype(jnp.bfloat16)
    return jnp.dot(active[None, :], weight, preferred_element_type=jnp.float32)[0]


def normalize(token_rows, shift_vec, scale_vec):
    values = token_rows.astype(jnp.float32)
    center = values - jnp.mean(values, axis=-1, keepdims=True)
    spread = jnp.mean(center * center, axis=-1, keepdims=True)
    return (center * lax.rsqrt(spread + EPS) * (1.0 + scale_vec) + shift_vec).astype(jnp.bfloat16)


def scores_of(query_heads, key_value, head_count):
    requests, key_count = (key_value.shape[0], key_value.shape[1])
    key_heads = key_value[:, :, 0].reshape(requests, key_count, head_count, HEAD)
    value_heads = key_value[:, :, 1].reshape(requests, key_count, head_count, HEAD)
    scores = jnp.einsum(
        "rqhe,rkhe->rhqk", query_heads, key_heads, preferred_element_type=jnp.float32
    ) * HEAD ** (-0.5)
    return (scores, value_heads)


def masked_max(scores, key_mask):
    return jnp.max(jnp.where(key_mask[:, None, None, :], scores, NEG), axis=-1)


def weighed(scores, key_mask, top_score, value_heads):
    weights = jnp.where(key_mask[:, None, None, :], jnp.exp(scores - top_score[..., None]), 0.0)
    weight_sum = jnp.sum(weights, axis=-1)
    accumulated = jnp.einsum(
        "rhqk,rkhe->rhqe",
        weights.astype(jnp.bfloat16),
        value_heads,
        preferred_element_type=jnp.float32,
    )
    return (weight_sum, accumulated)


def body(video, text, patch_lengths, text_len, timestep, w_mod, w_qkv, w_out, stale_cache):
    section_index = lax.axis_index("section")
    seq_count = lax.axis_size("seq")
    requests, patches, per_dev, model_width = video.shape
    text_dev = text.shape[1]
    capacity = per_dev * seq_count
    text_slots = text_dev * seq_count
    column_count = w_out.shape[1]
    head_count = column_count // HEAD
    row_count = per_dev + text_dev
    modulated = lax.all_gather(modulation(timestep, w_mod[0]), "mp", axis=0, tiled=True)
    shift_vec = modulated[:model_width]
    scale_vec = modulated[model_width : 2 * model_width]
    gate_vec = modulated[2 * model_width :]
    weight_qkv = w_qkv[0].reshape(model_width, 3 * column_count)
    weight_out = w_out[0]
    stale_local = stale_cache[0]
    slot_index = jnp.arange(capacity, dtype=jnp.int32)
    video_valid = (slot_index[None, None, :] < patch_lengths[:, :, None]).reshape(requests, -1)
    text_valid = jnp.arange(text_slots, dtype=jnp.int32)[None, :] < text_len[:, None]
    all_valid = jnp.concatenate([video_valid, text_valid], axis=1)
    video_patch = jnp.repeat(jnp.arange(patches, dtype=jnp.int32), capacity)
    all_patch = jnp.concatenate([video_patch, jnp.zeros((text_slots,), jnp.int32)])
    stale_whole = lax.all_gather(stale_local, "seq", axis=2, tiled=True).reshape(
        requests, patches * capacity, 2, column_count
    )
    fresh_video = jnp.zeros((requests, patches, capacity, 2, column_count), jnp.bfloat16)
    fresh_text = jnp.zeros((requests, text_slots, 2, column_count), jnp.bfloat16)
    own_video = jnp.zeros((requests, patches, per_dev, 2, column_count), jnp.bfloat16)
    own_text = jnp.zeros((requests, text_dev, 2, column_count), jnp.bfloat16)
    out_video = jnp.zeros((requests, patches, per_dev, model_width), jnp.bfloat16)
    out_text = jnp.zeros((requests, text_dev, model_width), jnp.bfloat16)
    received = jnp.zeros((requests, row_count, model_width), jnp.bfloat16)
    patch_ids = jnp.arange(patches, dtype=jnp.int32)
    for turn_index in range(patches + 1):
        patch_now = turn_index - section_index
        picked = lax.dynamic_index_in_dim(
            video, jnp.clip(patch_now, 0, patches - 1), 1, keepdims=False
        )
        token_rows = jnp.where(
            section_index == 0, jnp.concatenate([picked, text], axis=1), received
        )
        normed = normalize(token_rows, shift_vec, scale_vec)
        projected = jnp.dot(
            normed.reshape(-1, model_width), weight_qkv, preferred_element_type=jnp.float32
        )
        projected = projected.reshape(requests, row_count, 3, column_count).astype(jnp.bfloat16)
        queries = projected[:, :, 0]
        key_value = projected[:, :, 1:]
        gathered_video, gathered_text = (
            lax.all_gather(key_value[:, :per_dev], "seq", axis=1, tiled=True),
            lax.all_gather(key_value[:, per_dev:], "seq", axis=1, tiled=True),
        )
        current = patch_ids == patch_now
        fresh_video = jnp.where(
            current[None, :, None, None, None], gathered_video[:, None], fresh_video
        )
        fresh_text = jnp.where(patch_now == 0, gathered_text, fresh_text)
        own_video = jnp.where(
            current[None, :, None, None, None], key_value[:, None, :per_dev], own_video
        )
        own_text = jnp.where(patch_now == 0, key_value[:, per_dev:], own_text)
        fresh_all = jnp.concatenate(
            [fresh_video.reshape(requests, patches * capacity, 2, column_count), fresh_text], axis=1
        )
        fresh_mask = all_valid & (all_patch[None, :] <= patch_now)
        query_heads = queries.reshape(requests, row_count, head_count, HEAD)
        scores, value_heads = scores_of(query_heads, fresh_all, head_count)
        fresh_top = masked_max(scores, fresh_mask)
        fresh_sum, fresh_acc = weighed(scores, fresh_mask, fresh_top, value_heads)
        stale_mask = video_valid & (video_patch[None, :] > patch_now)
        scores, value_heads = scores_of(query_heads, stale_whole, head_count)
        stale_top = masked_max(scores, stale_mask)
        stale_sum, stale_acc = weighed(scores, stale_mask, stale_top, value_heads)
        top_score = jnp.maximum(fresh_top, stale_top)
        fresh_weight = jnp.exp(fresh_top - top_score)
        stale_weight = jnp.exp(stale_top - top_score)
        numer = fresh_acc * fresh_weight[..., None] + stale_acc * stale_weight[..., None]
        denom = fresh_sum * fresh_weight + stale_sum * stale_weight
        attended = (numer / denom[..., None]).astype(jnp.bfloat16)
        attended = attended.transpose(0, 2, 1, 3).reshape(requests * row_count, column_count)
        partial_out = jnp.dot(attended, weight_out, preferred_element_type=jnp.float32).reshape(
            requests, row_count, model_width
        )
        summed = lax.psum(partial_out, "mp")
        result = (token_rows.astype(jnp.float32) + gate_vec * summed).astype(jnp.bfloat16)
        out_video = jnp.where(current[None, :, None, None], result[:, None, :per_dev], out_video)
        out_text = jnp.where(patch_now == 0, result[:, per_dev:], out_text)
        if turn_index < patches:
            received = passed_along(result, "section", 1)
    return (out_video[None], out_text[None], own_video[None], own_text[None])


def solution(mesh):
    placed = (
        P(None, None, "seq", None),
        P(None, "seq", None),
        P(),
        P(),
        P(),
        P("section", None, "mp"),
        P("section", None, None, "mp"),
        P("section", "mp", None),
        P("section", None, None, "seq", None, "mp"),
    )
    return jax.shard_map(
        body,
        mesh=mesh,
        in_specs=placed,
        out_specs=(
            P("section", None, None, "seq", None),
            P("section", None, "seq", None),
            P("section", None, None, "seq", None, "mp"),
            P("section", None, "seq", None, "mp"),
        ),
        check_vma=False,
    )
```

profile of v0, /device:TPU:1, one launch (start us, length us, event | category | flops | bytes accessed | tf_op | source)
XLA Modules:
  0.0 716.3 jit_solution(2597853420989053191)
XLA Ops:
  8.0 18.7 %copy.75 = bf16[1,3072,3,768]{1,3,2,0:T(8,128)(2,1)} copy(bf16[1,3072,3,768]{3,1,2,0:T(8,128)(2,1)} %param.15) | data formatting | bytes 28311552 | tf_op args[6]
  27.8 6.4 all-gather.1
  35.4 9.3 %fusion.26 = bf16[2,16,3,768]{3,1,2,0:T(8,128)(2,1)S(1)} fusion(bf16[1,3072,3,768]{1,3,2,0:T(8,128)(2,1)} %copy.75, f32[3072]{0:T(1024)S(1)} %get-tuple-element.76, f32[3072]{0:T(1024)S(1)} %get-tuple-element.77, f32[2,16]{1,0:T(2,128)S(1)} %add_rsqrt_fusion.4, f32[2,16]{1,0:T(2,128)S(1)} %broadcast_multiply_fusion.4, ...), kind=kOutput, calls=%fused_computation.57 | convolution fusion | flops 454139904 | bytes 14524673 | tf_op jit(solution)/shard_map/dot_general | solution.py:103
  44.9 24.0 %all_gather.38 = bf16[2,128,2,768]{3,1,2,0:T(8,128)(2,1)S(1)} all-gather(bf16[2,8,2,768]{3,1,2,0:T(8,128)(2,1)S(1)} %get-tuple-element.73), channel_id=1, replica_groups=mesh['section'=2,'seq'=16,'mp'=4] {'seq'}, dimensions={1}, use_global_device_ids=true | all-gather | bytes 835584 | tf_op jit(solution)/shard_map/all_gather | solution.py:111
  70.1 17.7 %all_gather.37 = bf16[2,128,2,768]{3,1,2,0:T(8,128)(2,1)S(1)} all-gather(bf16[2,8,2,768]{3,1,2,0:T(8,128)(2,1)S(1)} %get-tuple-element.74), channel_id=1, replica_groups=mesh['section'=2,'seq'=16,'mp'=4] {'seq'}, dimensions={1}, use_global_device_ids=true | all-gather | bytes 835584 | tf_op jit(solution)/shard_map/all_gather | solution.py:110
  90.6 5.7 broadcast_in_dim.475
  102.9 9.3 %fusion.259 = (bf16[2,512,1,768]{3,2,1,0:T(2,128)(2,1)}, bf16[2,512,1,768]{3,2,1,0:T(2,128)(2,1)}) fusion(bf16[2,512,2,768]{3,2,1,0:T(2,128)(2,1)} %bitcast.353), kind=kLoop, calls=%fused_computation.383 | loop fusion | bytes 6291456 | tf_op jit(solution)/shard_map/slice | solution.py:36
  112.2 6.8 copy.115
  119.0 8.1 %copy.114 = bf16[2,512,1,768]{1,3,0,2:T(8,128)(2,1)} copy(bf16[2,512,1,768]{3,2,1,0:T(2,128)(2,1)} %get-tuple-element.51) | data formatting | bytes 3145728
  135.2 45.4 %all-reduce.7.cloned.1.call-done = f32[2,16,3072]{2,1,0:T(8,128)} async-done(((f32[2,16,3072]{2,1,0:T(8,128)}), f32[2,16,3072]{2,1,0:T(8,128)}) %all-reduce.7.cloned.1.call-update) | async-done | bytes 393232 | tf_op jit(solution)/shard_map/psum | solution.py:144
  181.7 4.3 collective-permute-start
  190.5 9.3 %fusion.29 = bf16[2,16,3,768]{3,1,2,0:T(8,128)(2,1)S(1)} fusion(bf16[1,3072,3,768]{1,3,2,0:T(8,128)(2,1)} %copy.75, bf16[2,16,3072]{2,1,0:T(8,128)(2,1)S(1)} %get-tuple-element.37, f32[2,16]{1,0:T(2,128)S(1)} %add_rsqrt_fusion.3, f32[2,16]{1,0:T(2,128)S(1)} %broadcast_multiply_fusion.3, f32[3072]{0:T(1024)S(1)} %get-tuple-element.76, ...), kind=kOutput, calls=%fused_computation.58 | convolution fusion | flops 453648384 | bytes 14524672 | tf_op jit(solution)/shard_map/dot_general | solution.py:103
  201.3 19.7 %all_gather.41 = bf16[2,128,2,768]{3,1,2,0:T(8,128)(2,1)S(1)} all-gather(bf16[2,8,2,768]{3,1,2,0:T(8,128)(2,1)S(1)} %get-tuple-element.71), channel_id=1, replica_groups=mesh['section'=2,'seq'=16,'mp'=4] {'seq'}, dimensions={1}, use_global_device_ids=true | all-gather | bytes 835584 | tf_op jit(solution)/shard_map/all_gather | solution.py:111
  222.3 19.1 %all_gather.40 = bf16[2,128,2,768]{3,1,2,0:T(8,128)(2,1)S(1)} all-gather(bf16[2,8,2,768]{3,1,2,0:T(8,128)(2,1)} %get-tuple-element.72), channel_id=1, replica_groups=mesh['section'=2,'seq'=16,'mp'=4] {'seq'}, dimensions={1}, use_global_device_ids=true | all-gather | bytes 835584 | tf_op jit(solution)/shard_map/all_gather | solution.py:110
  246.2 5.8 broadcast_in_dim.488
  264.9 47.4 %all-reduce.9.cloned.1.call-done = f32[2,16,3072]{2,1,0:T(8,128)} async-done(((f32[2,16,3072]{2,1,0:T(8,128)}), f32[2,16,3072]{2,1,0:T(8,128)}) %all-reduce.9.cloned.1.call-update) | async-done | bytes 393232 | tf_op jit(solution)/shard_map/psum | solution.py:144
  313.4 4.3 collective-permute-start.1
  322.2 9.3 %fusion.32 = bf16[2,16,3,768]{3,1,2,0:T(8,128)(2,1)S(1)} fusion(bf16[1,3072,3,768]{1,3,2,0:T(8,128)(2,1)} %copy.75, bf16[2,16,3072]{2,1,0:T(8,128)(2,1)S(1)} %get-tuple-element.32, f32[2,16]{1,0:T(2,128)S(1)} %add_rsqrt_fusion.2, f32[2,16]{1,0:T(2,128)S(1)} %broadcast_multiply_fusion.2, f32[3072]{0:T(1024)S(1)} %get-tuple-element.76, ...), kind=kOutput, calls=%fused_computation.59 | convolution fusion | flops 453648384 | bytes 14524672 | tf_op jit(solution)/shard_map/dot_general | solution.py:103
  333.6 19.7 %all_gather.43 = bf16[2,128,2,768]{3,1,2,0:T(8,128)(2,1)S(1)} all-gather(bf16[2,8,2,768]{3,1,2,0:T(8,128)(2,1)S(1)} %get-tuple-element.69), channel_id=1, replica_groups=mesh['section'=2,'seq'=16,'mp'=4] {'seq'}, dimensions={1}, use_global_device_ids=true | all-gather | bytes 835584 | tf_op jit(solution)/shard_map/all_gather | solution.py:111
  354.6 19.2 %all_gather.42 = bf16[2,128,2,768]{3,1,2,0:T(8,128)(2,1)S(1)} all-gather(bf16[2,8,2,768]{3,1,2,0:T(8,128)(2,1)} %get-tuple-element.70), channel_id=1, replica_groups=mesh['section'=2,'seq'=16,'mp'=4] {'seq'}, dimensions={1}, use_global_device_ids=true | all-gather | bytes 835584 | tf_op jit(solution)/shard_map/all_gather | solution.py:110
  378.5 5.7 broadcast_in_dim.495
  397.2 47.5 %all-reduce.11.cloned.1.call-done = f32[2,16,3072]{2,1,0:T(8,128)} async-done(((f32[2,16,3072]{2,1,0:T(8,128)}), f32[2,16,3072]{2,1,0:T(8,128)}) %all-reduce.11.cloned.1.call-update) | async-done | bytes 393232 | tf_op jit(solution)/shard_map/psum | solution.py:144
  454.6 9.3 %fusion.35 = bf16[2,16,3,768]{3,1,2,0:T(8,128)(2,1)S(1)} fusion(bf16[1,3072,3,768]{1,3,2,0:T(8,128)(2,1)} %copy.75, bf16[2,16,3072]{2,1,0:T(8,128)(2,1)S(1)} %get-tuple-element.27, f32[2,16]{1,0:T(2,128)S(1)} %add_rsqrt_fusion.1, f32[2,16]{1,0:T(2,128)S(1)} %broadcast_multiply_fusion.1, f32[3072]{0:T(1024)S(1)} %get-tuple-element.76, ...), kind=kOutput, calls=%fused_computation.60 | convolution fusion | flops 453648384 | bytes 14524672 | tf_op jit(solution)/shard_map/dot_general | solution.py:103
  465.4 19.7 %all_gather.45 = bf16[2,128,2,768]{3,1,2,0:T(8,128)(2,1)S(1)} all-gather(bf16[2,8,2,768]{3,1,2,0:T(8,128)(2,1)S(1)} %get-tuple-element.67), channel_id=1, replica_groups=mesh['section'=2,'seq'=16,'mp'=4] {'seq'}, dimensions={1}, use_global_device_ids=true | all-gather | bytes 835584 | tf_op jit(solution)/shard_map/all_gather | solution.py:111
  486.4 19.2 %all_gather.44 = bf16[2,128,2,768]{3,1,2,0:T(8,128)(2,1)S(1)} all-gather(bf16[2,8,2,768]{3,1,2,0:T(8,128)(2,1)} %get-tuple-element.68), channel_id=1, replica_groups=mesh['section'=2,'seq'=16,'mp'=4] {'seq'}, dimensions={1}, use_global_device_ids=true | all-gather | bytes 835584 | tf_op jit(solution)/shard_map/all_gather | solution.py:110
  510.4 5.8 broadcast_in_dim.502
  529.1 47.4 %all-reduce.13.cloned.1.call-done = f32[2,16,3072]{2,1,0:T(8,128)} async-done(((f32[2,16,3072]{2,1,0:T(8,128)}), f32[2,16,3072]{2,1,0:T(8,128)}) %all-reduce.13.cloned.1.call-update) | async-done | bytes 393232 | tf_op jit(solution)/shard_map/psum | solution.py:144
  586.4 9.3 %fusion.38 = bf16[2,16,3,768]{3,1,2,0:T(8,128)(2,1)S(1)} fusion(bf16[1,3072,3,768]{1,3,2,0:T(8,128)(2,1)} %copy.75, bf16[2,16,3072]{2,1,0:T(8,128)(2,1)S(1)} %get-tuple-element.22, f32[2,16]{1,0:T(2,128)S(1)} %add_rsqrt_fusion, f32[2,16]{1,0:T(2,128)S(1)} %broadcast_multiply_fusion, f32[3072]{0:T(1024)S(1)} %get-tuple-element.76, ...), kind=kOutput, calls=%fused_computation.61 | convolution fusion | flops 453648384 | bytes 14524672 | tf_op jit(solution)/shard_map/dot_general | solution.py:103
  597.4 19.7 %all_gather.47 = bf16[2,128,2,768]{3,1,2,0:T(8,128)(2,1)S(1)} all-gather(bf16[2,8,2,768]{3,1,2,0:T(8,128)(2,1)S(1)} %get-tuple-element.65), channel_id=1, replica_groups=mesh['section'=2,'seq'=16,'mp'=4] {'seq'}, dimensions={1}, use_global_device_ids=true | all-gather | bytes 835584 | tf_op jit(solution)/shard_map/all_gather | solution.py:111
  618.3 19.2 %all_gather.46 = bf16[2,128,2,768]{3,1,2,0:T(8,128)(2,1)S(1)} all-gather(bf16[2,8,2,768]{3,1,2,0:T(8,128)(2,1)} %get-tuple-element.66), channel_id=1, replica_groups=mesh['section'=2,'seq'=16,'mp'=4] {'seq'}, dimensions={1}, use_global_device_ids=true | all-gather | bytes 835584 | tf_op jit(solution)/shard_map/all_gather | solution.py:110
  640.4 5.7 broadcast_in_dim.509
  663.0 43.2 %all-reduce.15.cloned.1.call-done = f32[2,16,3072]{2,1,0:T(8,128)} async-done(((f32[2,16,3072]{2,1,0:T(8,128)}), f32[2,16,3072]{2,1,0:T(8,128)}) %all-reduce.15.cloned.1.call-update) | async-done | bytes 393232 | tf_op jit(solution)/shard_map/psum | solution.py:144
  (287 shorter events, 138.7 us)
Async XLA Ops:
  7.2 20.3 %copy-start = (bf16[1,512,2304]{2,1,0:T(8,128)(2,1)S(1)}, bf16[1,512,2304]{2,1,0:T(8,128)(2,1)}, u32[]{:S(2)}) copy-start(bf16[1,512,2304]{2,1,0:T(8,128)(2,1)} %param.14) | copy-start | bytes 7077892
  7.2 95.7 %all-gather.4.cloned.1.call-start = ((), (), s32[]{:S(2)}) async-start(), calls=%async_computation.5 | async-start | bytes 3342336 | tf_op jit(solution)/shard_map/all_gather | solution.py:83
  7.9 172.7 %all-reduce.7.cloned.1.call-start = ((), (), s32[]{:S(2)}) async-start(), calls=%async_computation | async-start | bytes 786432 | tf_op jit(solution)/shard_map/psum | solution.py:144
  8.0 26.3 %copy-start.34 = (bf16[2,4,8,3072]{3,2,1,0:T(8,128)(2,1)S(1)}, bf16[2,4,8,3072]{3,2,1,0:T(8,128)(2,1)}, u32[]{:S(2)}) copy-start(bf16[2,4,8,3072]{3,2,1,0:T(8,128)(2,1)} %param.9) | copy-start | bytes 1179652
  26.6 8.4 %copy-start.9 = (bf16[2,8,3072]{2,1,0:T(8,128)(2,1)S(1)}, bf16[2,8,3072]{2,1,0:T(8,128)(2,1)}, u32[]{:S(2)}) copy-start(bf16[2,8,3072]{2,1,0:T(8,128)(2,1)} %param.10) | copy-start | bytes 294916
  44.7 43.5 %copy-start.22 = (bf16[2,16,3,768]{3,1,2,0:T(8,128)(2,1)}, bf16[2,16,3,768]{3,1,2,0:T(8,128)(2,1)S(1)}, u32[]{:S(2)}) copy-start(bf16[2,16,3,768]{3,1,2,0:T(8,128)(2,1)S(1)} %fusion.26) | copy-start | bytes 442372
  44.9 56.1 %copy-start.18 = (bf16[2,16,12,64]{3,2,1,0:T(8,128)(2,1)}, bf16[2,16,12,64]{3,2,1,0:T(8,128)(2,1)S(1)}, u32[]{:S(2)}) copy-start(bf16[2,16,12,64]{3,2,1,0:T(8,128)(2,1)S(1)} %reshape_squeeze.63) | copy-start | bytes 147460
  131.0 59.1 %copy-start.40 = (bf16[2,8,3072]{2,1,0:T(8,128)(2,1)S(1)}, bf16[2,8,3072]{2,1,0:T(8,128)(2,1)}, u32[]{:S(2)}) copy-start(bf16[2,8,3072]{2,1,0:T(8,128)(2,1)} %get-tuple-element.57) | copy-start | bytes 294916
  135.1 177.3 %all-reduce.9.cloned.1.call-start = ((), (), s32[]{:S(2)}) async-start(), calls=%async_computation.1 | async-start | bytes 786432 | tf_op jit(solution)/shard_map/psum | solution.py:144
  135.2 55.0 %copy-start.46 = (pred[4]{0:T(512)(128)(4,1)}, pred[4]{0:T(512)(128)(4,1)S(1)}, u32[]{:S(2)}) copy-start(pred[4]{0:T(512)(128)(4,1)S(1)} %iota_compare_fusion.3) | copy-start | bytes 16
  181.7 8.8 %copy-start.26 = (bf16[2,16,3072]{2,1,0:T(8,128)(2,1)}, bf16[2,16,3072]{2,1,0:T(8,128)(2,1)S(1)}, u32[]{:S(2)}) copy-start(bf16[2,16,3072]{2,1,0:T(8,128)(2,1)S(1)} %fusion.136) | copy-start | bytes 589828
  181.7 8.4 %collective-permute-start = (bf16[2,16,3072]{2,1,0:T(8,128)(2,1)S(1)}, bf16[2,16,3072]{2,1,0:T(8,128)(2,1)S(1)}, u32[]{:S(2)}, u32[]{:S(2)}) collective-permute-start(bf16[2,16,3072]{2,1,0:T(8,128)(2,1)S(1)} %fusion.136), channel_id=1, source_target_pairs={{0,64},{1,65},{2,66},{3,67},{4,68},{5,69},{6,70},{7,71},{8,72},{9,... | collective-permute-start | bytes 589832 | tf_op jit(solution)/shard_map/ppermute | solution.py:15
  260.8 61.1 %copy-start.39 = (bf16[2,8,3072]{2,1,0:T(8,128)(2,1)S(1)}, bf16[2,8,3072]{2,1,0:T(8,128)(2,1)}, u32[]{:S(2)}) copy-start(bf16[2,8,3072]{2,1,0:T(8,128)(2,1)} %get-tuple-element.54) | copy-start | bytes 294916
  264.8 179.9 %all-reduce.11.cloned.1.call-start = ((), (), s32[]{:S(2)}) async-start(), calls=%async_computation.2 | async-start | bytes 786432 | tf_op jit(solution)/shard_map/psum | solution.py:144
  264.9 57.1 %copy-start.48 = (pred[4]{0:T(512)(128)(4,1)}, pred[4]{0:T(512)(128)(4,1)S(1)}, u32[]{:S(2)}) copy-start(pred[4]{0:T(512)(128)(4,1)S(1)} %iota_compare_fusion.2) | copy-start | bytes 16
  313.4 8.8 %copy-start.28 = (bf16[2,16,3072]{2,1,0:T(8,128)(2,1)}, bf16[2,16,3072]{2,1,0:T(8,128)(2,1)S(1)}, u32[]{:S(2)}) copy-start(bf16[2,16,3072]{2,1,0:T(8,128)(2,1)S(1)} %fusion.137) | copy-start | bytes 589828
  313.4 8.4 %collective-permute-start.1 = (bf16[2,16,3072]{2,1,0:T(8,128)(2,1)S(1)}, bf16[2,16,3072]{2,1,0:T(8,128)(2,1)S(1)}, u32[]{:S(2)}, u32[]{:S(2)}) collective-permute-start(bf16[2,16,3072]{2,1,0:T(8,128)(2,1)S(1)} %fusion.137), channel_id=1, source_target_pairs={{0,64},{1,65},{2,66},{3,67},{4,68},{5,69},{6,70},{7,71},{8,72},{9,... | collective-permute-start | bytes 589832 | tf_op jit(solution)/shard_map/ppermute | solution.py:15
  393.1 61.2 %copy-start.38 = (bf16[2,8,3072]{2,1,0:T(8,128)(2,1)S(1)}, bf16[2,8,3072]{2,1,0:T(8,128)(2,1)}, u32[]{:S(2)}) copy-start(bf16[2,8,3072]{2,1,0:T(8,128)(2,1)} %get-tuple-element.55) | copy-start | bytes 294916
  397.1 179.4 %all-reduce.13.cloned.1.call-start = ((), (), s32[]{:S(2)}) async-start(), calls=%async_computation.3 | async-start | bytes 786432 | tf_op jit(solution)/shard_map/psum | solution.py:144
  445.8 8.8 %copy-start.30 = (bf16[2,16,3072]{2,1,0:T(8,128)(2,1)}, bf16[2,16,3072]{2,1,0:T(8,128)(2,1)S(1)}, u32[]{:S(2)}) copy-start(bf16[2,16,3072]{2,1,0:T(8,128)(2,1)S(1)} %fusion.138) | copy-start | bytes 589828
  445.8 8.4 %collective-permute-start.2 = (bf16[2,16,3072]{2,1,0:T(8,128)(2,1)S(1)}, bf16[2,16,3072]{2,1,0:T(8,128)(2,1)S(1)}, u32[]{:S(2)}, u32[]{:S(2)}) collective-permute-start(bf16[2,16,3072]{2,1,0:T(8,128)(2,1)S(1)} %fusion.138), channel_id=1, source_target_pairs={{0,64},{1,65},{2,66},{3,67},{4,68},{5,69},{6,70},{7,71},{8,72},{9,... | collective-permute-start | bytes 589832 | tf_op jit(solution)/shard_map/ppermute | solution.py:15
  524.9 61.1 %copy-start.37 = (bf16[2,8,3072]{2,1,0:T(8,128)(2,1)S(1)}, bf16[2,8,3072]{2,1,0:T(8,128)(2,1)}, u32[]{:S(2)}) copy-start(bf16[2,8,3072]{2,1,0:T(8,128)(2,1)} %get-tuple-element.53) | copy-start | bytes 294916
  529.0 177.2 %all-reduce.15.cloned.1.call-start = ((), (), s32[]{:S(2)}) async-start(), calls=%async_computation.4 | async-start | bytes 786432 | tf_op jit(solution)/shard_map/psum | solution.py:144
  577.6 8.6 %copy-start.32 = (bf16[2,16,3072]{2,1,0:T(8,128)(2,1)}, bf16[2,16,3072]{2,1,0:T(8,128)(2,1)S(1)}, u32[]{:S(2)}) copy-start(bf16[2,16,3072]{2,1,0:T(8,128)(2,1)S(1)} %fusion.139) | copy-start | bytes 589828
  577.6 8.4 %collective-permute-start.3 = (bf16[2,16,3072]{2,1,0:T(8,128)(2,1)S(1)}, bf16[2,16,3072]{2,1,0:T(8,128)(2,1)S(1)}, u32[]{:S(2)}, u32[]{:S(2)}) collective-permute-start(bf16[2,16,3072]{2,1,0:T(8,128)(2,1)S(1)} %fusion.139), channel_id=1, source_target_pairs={{0,64},{1,65},{2,66},{3,67},{4,68},{5,69},{6,70},{7,71},{8,72},{9,... | collective-permute-start | bytes 589832 | tf_op jit(solution)/shard_map/ppermute | solution.py:15
  654.4 7.6 %copy-start.45 = (pred[4]{0:T(512)(128)(4,1)S(1)}, pred[4]{0:T(512)(128)(4,1)}, u32[]{:S(2)}) copy-start(pred[4]{0:T(512)(128)(4,1)} %copy-done.44) | copy-start | bytes 16
  654.4 7.6 %copy-start.47 = (pred[4]{0:T(512)(128)(4,1)S(1)}, pred[4]{0:T(512)(128)(4,1)}, u32[]{:S(2)}) copy-start(pred[4]{0:T(512)(128)(4,1)} %copy-done.46) | copy-start | bytes 16
  654.4 52.9 %copy-start.27 = (bf16[2,16,3072]{2,1,0:T(8,128)(2,1)S(1)}, bf16[2,16,3072]{2,1,0:T(8,128)(2,1)}, u32[]{:S(2)}) copy-start(bf16[2,16,3072]{2,1,0:T(8,128)(2,1)} %copy-done.26) | copy-start | bytes 589828
  654.4 52.9 %copy-start.29 = (bf16[2,16,3072]{2,1,0:T(8,128)(2,1)S(1)}, bf16[2,16,3072]{2,1,0:T(8,128)(2,1)}, u32[]{:S(2)}) copy-start(bf16[2,16,3072]{2,1,0:T(8,128)(2,1)} %copy-done.28) | copy-start | bytes 589828
  654.4 52.9 %copy-start.31 = (bf16[2,16,3072]{2,1,0:T(8,128)(2,1)S(1)}, bf16[2,16,3072]{2,1,0:T(8,128)(2,1)}, u32[]{:S(2)}) copy-start(bf16[2,16,3072]{2,1,0:T(8,128)(2,1)} %copy-done.30) | copy-start | bytes 589828
  654.4 52.9 %copy-start.33 = (bf16[2,16,3072]{2,1,0:T(8,128)(2,1)S(1)}, bf16[2,16,3072]{2,1,0:T(8,128)(2,1)}, u32[]{:S(2)}) copy-start(bf16[2,16,3072]{2,1,0:T(8,128)(2,1)} %copy-done.32) | copy-start | bytes 589828
  654.4 54.5 %copy-start.1 = (bf16[1,512,2304]{2,1,0:T(8,128)(2,1)S(1)}, bf16[1,512,2304]{2,1,0:T(8,128)(2,1)}, u32[]{:S(2)}) copy-start(bf16[1,512,2304]{2,1,0:T(8,128)(2,1)} %param.14) | copy-start | bytes 7077892
  (34 other events, 87.0 us)
Sparse Core Ops, SparseCore 0:
  10.2 52.0 all-gather.3
  135.2 45.3 all-reduce.6
  264.9 47.3 all-reduce.8
  397.3 47.4 all-reduce.10
  529.1 47.3 all-reduce.12
  658.8 47.4 all-reduce.14
where the time goes:
time: 723 us; the launch traced here: 716 us
  waiting for transfers between devices  246 us (34%)
  blocking collectives  203 us (28%)
  local copies, waits for them, and re-layouts  116 us (16%)
  matrix products  86.7 us (12%)
  other arithmetic  30.2 us (4%)
  starting transfers between devices  17.5 us (2%)
  between operations  16.3 us (2%)
    psum x5, waiting for transfers between devices, body(): summed = lax.psum(partial_out, 'mp')  231 us
    all_gather x5, blocking collectives, body(): lax.all_gather(key_value[:, per_dev:], 'seq', axis=1, tiled=True)  103 us
    all_gather x5, blocking collectives, body(): lax.all_gather(key_value[:, :per_dev], 'seq', axis=1, tiled=True)  94.4 us
    broadcast_in_dim x15, local copies, waits for them, and re-layouts, body(): jnp.where(current[None, :, None, None, None], gathered_video[:, None], fr...  47 us
    dot_general x5, matrix products, body(): jnp.dot(normed.reshape(-1, model_width), weight_qkv, preferred_element_ty...  46.6 us
    unnamed x117, local copies, waits for them, and re-layouts  41 us
    dot_general x5, matrix products, body(): jnp.dot(attended, weight_out, preferred_element_type=jnp.float32)  20.3 us
    ppermute x4, starting transfers between devices, passed_along(): lax.ppermute(value, axis, [(source, source + steps) for source in range(l...  17.3 us
  transfers between devices with their start and end apart: 10, of which 9 were waited for; matrix products, arithmetic and copies ran while one was open for 7% of the time, Pallas kernels for 0%

commit v1 on v0

--- a/solution.py
+++ b/solution.py
@@ -141,7 +141,7 @@
         partial_out = jnp.dot(attended, weight_out, preferred_element_type=jnp.float32).reshape(
             requests, row_count, model_width
         )
-        summed = lax.psum(partial_out, "mp")
+        summed = jnp.sum(lax.all_gather(partial_out, "mp"), axis=0)
         result = (token_rows.astype(jnp.float32) + gate_vec * summed).astype(jnp.bfloat16)
         out_video = jnp.where(current[None, :, None, None], result[:, None, :per_dev], out_video)
         out_text = jnp.where(patch_now == 0, result[:, per_dev:], out_text)

time: 723 us -> 665 us (0.920)
  waiting for transfers between devices: 246 us -> 189 us
    psum x5 -> x0, waiting for transfers between devices: 231 us -> none  [body(): summed = lax.psum(partial_out, 'mp')]
    all_gather x0 -> x5, waiting for transfers between devices: none -> 172 us  [body(): summed = jnp.sum(lax.all_gather(partial_out, 'mp'), axis=0)]
    reduce_sum x0 -> x5, other arithmetic: none -> 7.81 us  [body(): summed = jnp.sum(lax.all_gather(partial_out, 'mp'), axis=0)]
    unnamed x117 -> x145, local copies, waits for them, and re-layouts: 41 us -> 41.5 us
where the time goes in v1:
time: 665 us; the launch traced here: 658 us
  blocking collectives  203 us (31%)
  waiting for transfers between devices  189 us (28%)
  local copies, waits for them, and re-layouts  110 us (17%)
  matrix products  86.4 us (13%)
  other arithmetic  35.2 us (5%)
  starting transfers between devices  17.5 us (3%)
  between operations  16.3 us (2%)
    all_gather x5, waiting for transfers between devices, body(): summed = jnp.sum(lax.all_gather(partial_out, 'mp'), axis=0)  172 us
    all_gather x5, blocking collectives, body(): lax.all_gather(key_value[:, per_dev:], 'seq', axis=1, tiled=True)  103 us
    all_gather x5, blocking collectives, body(): lax.all_gather(key_value[:, :per_dev], 'seq', axis=1, tiled=True)  94.2 us
    dot_general x5, matrix products, body(): jnp.dot(normed.reshape(-1, model_width), weight_qkv, preferred_element_ty...  46.6 us
    broadcast_in_dim x15, local copies, waits for them, and re-layouts, body(): jnp.where(current[None, :, None, None, None], gathered_video[:, None], fr...  44.7 us
    unnamed x145, local copies, waits for them, and re-layouts  41.5 us
    dot_general x5, matrix products, body(): jnp.dot(attended, weight_out, preferred_element_type=jnp.float32)  20.1 us
    ppermute x4, starting transfers between devices, passed_along(): lax.ppermute(value, axis, [(source, source + steps) for source in range(l...  17.3 us
  transfers between devices with their start and end apart: 10, of which 9 were waited for; matrix products, arithmetic and copies ran while one was open for 7% of the time, Pallas kernels for 0%

profile of v1, /device:TPU:1, one launch (start us, length us, event | category | flops | bytes accessed | tf_op | source)
XLA Modules:
  0.0 658.0 jit_solution(17361726341779367216)
XLA Ops:
  8.0 18.7 %copy.75 = bf16[1,3072,3,768]{1,3,2,0:T(8,128)(2,1)} copy(bf16[1,3072,3,768]{3,1,2,0:T(8,128)(2,1)} %param.15) | data formatting | bytes 28311552 | tf_op args[6]
  27.9 6.4 all-gather.6
  35.4 9.3 %fusion.26 = bf16[2,16,3,768]{3,1,2,0:T(8,128)(2,1)S(1)} fusion(bf16[1,3072,3,768]{1,3,2,0:T(8,128)(2,1)} %copy.75, f32[3072]{0:T(1024)S(1)} %get-tuple-element.76, f32[3072]{0:T(1024)S(1)} %get-tuple-element.77, f32[2,16]{1,0:T(2,128)S(1)} %add_rsqrt_fusion.4, f32[2,16]{1,0:T(2,128)S(1)} %broadcast_multiply_fusion.4, ...), kind=kOutput, calls=%fused_computation.57 | convolution fusion | flops 454139904 | bytes 14524673 | tf_op jit(solution)/shard_map/dot_general | solution.py:103
  44.9 23.9 %all_gather.53 = bf16[2,128,2,768]{3,1,2,0:T(8,128)(2,1)S(1)} all-gather(bf16[2,8,2,768]{3,1,2,0:T(8,128)(2,1)S(1)} %get-tuple-element.73), channel_id=1, replica_groups=mesh['section'=2,'seq'=16,'mp'=4] {'seq'}, dimensions={1}, use_global_device_ids=true | all-gather | bytes 835584 | tf_op jit(solution)/shard_map/all_gather | solution.py:111
  70.1 17.4 %all_gather.52 = bf16[2,128,2,768]{3,1,2,0:T(8,128)(2,1)S(1)} all-gather(bf16[2,8,2,768]{3,1,2,0:T(8,128)(2,1)S(1)} %get-tuple-element.74), channel_id=1, replica_groups=mesh['section'=2,'seq'=16,'mp'=4] {'seq'}, dimensions={1}, use_global_device_ids=true | all-gather | bytes 835584 | tf_op jit(solution)/shard_map/all_gather | solution.py:110
  90.4 5.7 broadcast_in_dim.475
  103.1 9.4 %fusion.259 = (bf16[2,512,1,768]{3,2,1,0:T(2,128)(2,1)}, bf16[2,512,1,768]{3,2,1,0:T(2,128)(2,1)}) fusion(bf16[2,512,2,768]{3,2,1,0:T(2,128)(2,1)} %bitcast.358), kind=kLoop, calls=%fused_computation.383 | loop fusion | bytes 6291456 | tf_op jit(solution)/shard_map/slice | solution.py:36
  112.5 6.8 %copy.115 = bf16[2,512,1,768]{1,3,0,2:T(8,128)(2,1)S(1)} copy(bf16[2,512,1,768]{3,2,1,0:T(2,128)(2,1)} %get-tuple-element.52) | data formatting | bytes 3145728
  119.3 8.2 %copy.114 = bf16[2,512,1,768]{1,3,0,2:T(8,128)(2,1)} copy(bf16[2,512,1,768]{3,2,1,0:T(2,128)(2,1)} %get-tuple-element.51) | data formatting | bytes 3145728
  136.3 33.3 %all-gather.16.cloned.1.call-done = f32[8,16,3072]{2,1,0:T(8,128)} async-done(((f32[2,16,3072]{2,1,0:T(8,128)}), f32[8,16,3072]{2,1,0:T(8,128)}) %all-gather.16.cloned.1.call-update) | async-done | bytes 1572880 | tf_op jit(solution)/shard_map/all_gather | solution.py:144
  171.2 4.3 collective-permute-start
  180.0 9.3 %fusion.29 = bf16[2,16,3,768]{3,1,2,0:T(8,128)(2,1)S(1)} fusion(bf16[1,3072,3,768]{1,3,2,0:T(8,128)(2,1)} %copy.75, bf16[2,16,3072]{2,1,0:T(8,128)(2,1)S(1)} %get-tuple-element.37, f32[2,16]{1,0:T(2,128)S(1)} %add_rsqrt_fusion.3, f32[2,16]{1,0:T(2,128)S(1)} %broadcast_multiply_fusion.3, f32[3072]{0:T(1024)S(1)} %get-tuple-element.76, ...), kind=kOutput, calls=%fused_computation.58 | convolution fusion | flops 453648384 | bytes 14524672 | tf_op jit(solution)/shard_map/dot_general | solution.py:103
  190.2 19.7 %all_gather.57 = bf16[2,128,2,768]{3,1,2,0:T(8,128)(2,1)S(1)} all-gather(bf16[2,8,2,768]{3,1,2,0:T(8,128)(2,1)S(1)} %get-tuple-element.71), channel_id=1, replica_groups=mesh['section'=2,'seq'=16,'mp'=4] {'seq'}, dimensions={1}, use_global_device_ids=true | all-gather | bytes 835584 | tf_op jit(solution)/shard_map/all_gather | solution.py:111
  211.2 19.2 %all_gather.56 = bf16[2,128,2,768]{3,1,2,0:T(8,128)(2,1)S(1)} all-gather(bf16[2,8,2,768]{3,1,2,0:T(8,128)(2,1)S(1)} %get-tuple-element.72), channel_id=1, replica_groups=mesh['section'=2,'seq'=16,'mp'=4] {'seq'}, dimensions={1}, use_global_device_ids=true | all-gather | bytes 835584 | tf_op jit(solution)/shard_map/all_gather | solution.py:110
  235.2 5.7 broadcast_in_dim.488
  253.8 35.2 %all-gather.18.cloned.1.call-done = f32[8,16,3072]{2,1,0:T(8,128)} async-done(((f32[2,16,3072]{2,1,0:T(8,128)}), f32[8,16,3072]{2,1,0:T(8,128)}) %all-gather.18.cloned.1.call-update) | async-done | bytes 1572880 | tf_op jit(solution)/shard_map/all_gather | solution.py:144
  290.6 4.3 collective-permute-start.1
  299.4 9.3 %fusion.32 = bf16[2,16,3,768]{3,1,2,0:T(8,128)(2,1)S(1)} fusion(bf16[1,3072,3,768]{1,3,2,0:T(8,128)(2,1)} %copy.75, bf16[2,16,3072]{2,1,0:T(8,128)(2,1)S(1)} %get-tuple-element.32, f32[2,16]{1,0:T(2,128)S(1)} %add_rsqrt_fusion.2, f32[2,16]{1,0:T(2,128)S(1)} %broadcast_multiply_fusion.2, f32[3072]{0:T(1024)S(1)} %get-tuple-element.76, ...), kind=kOutput, calls=%fused_computation.59 | convolution fusion | flops 453648384 | bytes 14524672 | tf_op jit(solution)/shard_map/dot_general | solution.py:103
  310.2 19.7 %all_gather.60 = bf16[2,128,2,768]{3,1,2,0:T(8,128)(2,1)S(1)} all-gather(bf16[2,8,2,768]{3,1,2,0:T(8,128)(2,1)S(1)} %get-tuple-element.69), channel_id=1, replica_groups=mesh['section'=2,'seq'=16,'mp'=4] {'seq'}, dimensions={1}, use_global_device_ids=true | all-gather | bytes 835584 | tf_op jit(solution)/shard_map/all_gather | solution.py:111
  331.2 19.4 %all_gather.59 = bf16[2,128,2,768]{3,1,2,0:T(8,128)(2,1)S(1)} all-gather(bf16[2,8,2,768]{3,1,2,0:T(8,128)(2,1)S(1)} %get-tuple-element.70), channel_id=1, replica_groups=mesh['section'=2,'seq'=16,'mp'=4] {'seq'}, dimensions={1}, use_global_device_ids=true | all-gather | bytes 835584 | tf_op jit(solution)/shard_map/all_gather | solution.py:110
  355.3 5.7 broadcast_in_dim.495
  374.0 35.2 %all-gather.20.cloned.1.call-done = f32[8,16,3072]{2,1,0:T(8,128)} async-done(((f32[2,16,3072]{2,1,0:T(8,128)}), f32[8,16,3072]{2,1,0:T(8,128)}) %all-gather.20.cloned.1.call-update) | async-done | bytes 1572880 | tf_op jit(solution)/shard_map/all_gather | solution.py:144
  419.6 9.3 %fusion.35 = bf16[2,16,3,768]{3,1,2,0:T(8,128)(2,1)S(1)} fusion(bf16[1,3072,3,768]{1,3,2,0:T(8,128)(2,1)} %copy.75, bf16[2,16,3072]{2,1,0:T(8,128)(2,1)S(1)} %get-tuple-element.27, f32[2,16]{1,0:T(2,128)S(1)} %add_rsqrt_fusion.1, f32[2,16]{1,0:T(2,128)S(1)} %broadcast_multiply_fusion.1, f32[3072]{0:T(1024)S(1)} %get-tuple-element.76, ...), kind=kOutput, calls=%fused_computation.60 | convolution fusion | flops 453648384 | bytes 14524672 | tf_op jit(solution)/shard_map/dot_general | solution.py:103
  429.8 19.7 %all_gather.63 = bf16[2,128,2,768]{3,1,2,0:T(8,128)(2,1)S(1)} all-gather(bf16[2,8,2,768]{3,1,2,0:T(8,128)(2,1)S(1)} %get-tuple-element.67), channel_id=1, replica_groups=mesh['section'=2,'seq'=16,'mp'=4] {'seq'}, dimensions={1}, use_global_device_ids=true | all-gather | bytes 835584 | tf_op jit(solution)/shard_map/all_gather | solution.py:111
  450.8 19.1 %all_gather.62 = bf16[2,128,2,768]{3,1,2,0:T(8,128)(2,1)S(1)} all-gather(bf16[2,8,2,768]{3,1,2,0:T(8,128)(2,1)S(1)} %get-tuple-element.68), channel_id=1, replica_groups=mesh['section'=2,'seq'=16,'mp'=4] {'seq'}, dimensions={1}, use_global_device_ids=true | all-gather | bytes 835584 | tf_op jit(solution)/shard_map/all_gather | solution.py:110
  474.7 5.8 broadcast_in_dim.502
  493.3 35.2 %all-gather.22.cloned.1.call-done = f32[8,16,3072]{2,1,0:T(8,128)} async-done(((f32[2,16,3072]{2,1,0:T(8,128)}), f32[8,16,3072]{2,1,0:T(8,128)}) %all-gather.22.cloned.1.call-update) | async-done | bytes 1572880 | tf_op jit(solution)/shard_map/all_gather | solution.py:144
  538.9 9.3 %fusion.38 = bf16[2,16,3,768]{3,1,2,0:T(8,128)(2,1)S(1)} fusion(bf16[1,3072,3,768]{1,3,2,0:T(8,128)(2,1)} %copy.75, bf16[2,16,3072]{2,1,0:T(8,128)(2,1)S(1)} %get-tuple-element.22, f32[2,16]{1,0:T(2,128)S(1)} %add_rsqrt_fusion, f32[2,16]{1,0:T(2,128)S(1)} %broadcast_multiply_fusion, f32[3072]{0:T(1024)S(1)} %get-tuple-element.76, ...), kind=kOutput, calls=%fused_computation.61 | convolution fusion | flops 453648384 | bytes 14524672 | tf_op jit(solution)/shard_map/dot_general | solution.py:103
  549.9 19.7 %all_gather.66 = bf16[2,128,2,768]{3,1,2,0:T(8,128)(2,1)S(1)} all-gather(bf16[2,8,2,768]{3,1,2,0:T(8,128)(2,1)S(1)} %get-tuple-element.65), channel_id=1, replica_groups=mesh['section'=2,'seq'=16,'mp'=4] {'seq'}, dimensions={1}, use_global_device_ids=true | all-gather | bytes 835584 | tf_op jit(solution)/shard_map/all_gather | solution.py:111
  570.9 19.2 %all_gather.65 = bf16[2,128,2,768]{3,1,2,0:T(8,128)(2,1)S(1)} all-gather(bf16[2,8,2,768]{3,1,2,0:T(8,128)(2,1)S(1)} %get-tuple-element.66), channel_id=1, replica_groups=mesh['section'=2,'seq'=16,'mp'=4] {'seq'}, dimensions={1}, use_global_device_ids=true | all-gather | bytes 835584 | tf_op jit(solution)/shard_map/all_gather | solution.py:110
  592.9 5.7 broadcast_in_dim.509
  612.7 33.2 %all-gather.24.cloned.1.call-done = f32[8,16,3072]{2,1,0:T(8,128)} async-done(((f32[2,16,3072]{2,1,0:T(8,128)}), f32[8,16,3072]{2,1,0:T(8,128)}) %all-gather.24.cloned.1.call-update) | async-done | bytes 1572880 | tf_op jit(solution)/shard_map/all_gather | solution.py:144
  (320 shorter events, 139.5 us)
Async XLA Ops:
  7.2 20.3 %copy-start = (bf16[1,512,2304]{2,1,0:T(8,128)(2,1)S(1)}, bf16[1,512,2304]{2,1,0:T(8,128)(2,1)}, u32[]{:S(2)}) copy-start(bf16[1,512,2304]{2,1,0:T(8,128)(2,1)} %param.14) | copy-start | bytes 7077892
  7.2 95.9 %all-gather.14.cloned.1.call-start = ((), (), s32[]{:S(2)}) async-start(), calls=%async_computation | async-start | bytes 3342336 | tf_op jit(solution)/shard_map/all_gather | solution.py:83
  7.9 161.6 %all-gather.16.cloned.1.call-start = ((), (), s32[]{:S(2)}) async-start(), calls=%async_computation.1 | async-start | bytes 1966080 | tf_op jit(solution)/shard_map/all_gather | solution.py:144
  44.7 42.8 %copy-start.22 = (bf16[2,16,3,768]{3,1,2,0:T(8,128)(2,1)}, bf16[2,16,3,768]{3,1,2,0:T(8,128)(2,1)S(1)}, u32[]{:S(2)}) copy-start(bf16[2,16,3,768]{3,1,2,0:T(8,128)(2,1)S(1)} %fusion.26) | copy-start | bytes 442372
  44.9 55.8 %copy-start.18 = (bf16[2,16,12,64]{3,2,1,0:T(8,128)(2,1)}, bf16[2,16,12,64]{3,2,1,0:T(8,128)(2,1)S(1)}, u32[]{:S(2)}) copy-start(bf16[2,16,12,64]{3,2,1,0:T(8,128)(2,1)S(1)} %reshape_squeeze.63) | copy-start | bytes 147460
  44.9 42.6 %copy-start.34 = (bf16[2,8,2,768]{3,1,2,0:T(8,128)(2,1)}, bf16[2,8,2,768]{3,1,2,0:T(8,128)(2,1)S(1)}, u32[]{:S(2)}) copy-start(bf16[2,8,2,768]{3,1,2,0:T(8,128)(2,1)S(1)} %get-tuple-element.74) | copy-start | bytes 147460
  136.2 43.4 %copy-start.47 = (bf16[2,8,3072]{2,1,0:T(8,128)(2,1)S(1)}, bf16[2,8,3072]{2,1,0:T(8,128)(2,1)}, u32[]{:S(2)}) copy-start(bf16[2,8,3072]{2,1,0:T(8,128)(2,1)} %get-tuple-element.57) | copy-start | bytes 294916
  136.2 152.8 %all-gather.18.cloned.1.call-start = ((), (), s32[]{:S(2)}) async-start(), calls=%async_computation.2 | async-start | bytes 1966080 | tf_op jit(solution)/shard_map/all_gather | solution.py:144
  136.3 43.4 %copy-start.60 = (pred[4]{0:T(512)(128)(4,1)}, pred[4]{0:T(512)(128)(4,1)S(1)}, u32[]{:S(2)}) copy-start(pred[4]{0:T(512)(128)(4,1)S(1)} %iota_compare_fusion.3) | copy-start | bytes 16
  171.2 18.1 %copy-start.26 = (bf16[2,16,3072]{2,1,0:T(8,128)(2,1)}, bf16[2,16,3072]{2,1,0:T(8,128)(2,1)S(1)}, u32[]{:S(2)}) copy-start(bf16[2,16,3072]{2,1,0:T(8,128)(2,1)S(1)} %fusion.136) | copy-start | bytes 589828
  171.2 8.4 %collective-permute-start = (bf16[2,16,3072]{2,1,0:T(8,128)(2,1)S(1)}, bf16[2,16,3072]{2,1,0:T(8,128)(2,1)S(1)}, u32[]{:S(2)}, u32[]{:S(2)}) collective-permute-start(bf16[2,16,3072]{2,1,0:T(8,128)(2,1)S(1)} %fusion.136), channel_id=1, source_target_pairs={{0,64},{1,65},{2,66},{3,67},{4,68},{5,69},{6,70},{7,71},{8,72},{9,... | collective-permute-start | bytes 589832 | tf_op jit(solution)/shard_map/ppermute | solution.py:15
  189.4 21.8 %copy-start.36 = (bf16[2,8,2,768]{3,1,2,0:T(8,128)(2,1)}, bf16[2,8,2,768]{3,1,2,0:T(8,128)(2,1)S(1)}, u32[]{:S(2)}) copy-start(bf16[2,8,2,768]{3,1,2,0:T(8,128)(2,1)S(1)} %get-tuple-element.72) | copy-start | bytes 147460
  253.7 45.3 %copy-start.46 = (bf16[2,8,3072]{2,1,0:T(8,128)(2,1)S(1)}, bf16[2,8,3072]{2,1,0:T(8,128)(2,1)}, u32[]{:S(2)}) copy-start(bf16[2,8,3072]{2,1,0:T(8,128)(2,1)} %get-tuple-element.54) | copy-start | bytes 294916
  253.7 155.5 %all-gather.20.cloned.1.call-start = ((), (), s32[]{:S(2)}) async-start(), calls=%async_computation.3 | async-start | bytes 1966080 | tf_op jit(solution)/shard_map/all_gather | solution.py:144
  253.8 45.4 %copy-start.62 = (pred[4]{0:T(512)(128)(4,1)}, pred[4]{0:T(512)(128)(4,1)S(1)}, u32[]{:S(2)}) copy-start(pred[4]{0:T(512)(128)(4,1)S(1)} %iota_compare_fusion.2) | copy-start | bytes 16
  290.6 18.1 %copy-start.28 = (bf16[2,16,3072]{2,1,0:T(8,128)(2,1)}, bf16[2,16,3072]{2,1,0:T(8,128)(2,1)S(1)}, u32[]{:S(2)}) copy-start(bf16[2,16,3072]{2,1,0:T(8,128)(2,1)S(1)} %fusion.137) | copy-start | bytes 589828
  290.6 8.4 %collective-permute-start.1 = (bf16[2,16,3072]{2,1,0:T(8,128)(2,1)S(1)}, bf16[2,16,3072]{2,1,0:T(8,128)(2,1)S(1)}, u32[]{:S(2)}, u32[]{:S(2)}) collective-permute-start(bf16[2,16,3072]{2,1,0:T(8,128)(2,1)S(1)} %fusion.137), channel_id=1, source_target_pairs={{0,64},{1,65},{2,66},{3,67},{4,68},{5,69},{6,70},{7,71},{8,72},{9,... | collective-permute-start | bytes 589832 | tf_op jit(solution)/shard_map/ppermute | solution.py:15
  309.4 21.8 %copy-start.38 = (bf16[2,8,2,768]{3,1,2,0:T(8,128)(2,1)}, bf16[2,8,2,768]{3,1,2,0:T(8,128)(2,1)S(1)}, u32[]{:S(2)}) copy-start(bf16[2,8,2,768]{3,1,2,0:T(8,128)(2,1)S(1)} %get-tuple-element.70) | copy-start | bytes 147460
  373.9 45.3 %copy-start.45 = (bf16[2,8,3072]{2,1,0:T(8,128)(2,1)S(1)}, bf16[2,8,3072]{2,1,0:T(8,128)(2,1)}, u32[]{:S(2)}) copy-start(bf16[2,8,3072]{2,1,0:T(8,128)(2,1)} %get-tuple-element.55) | copy-start | bytes 294916
  373.9 154.6 %all-gather.22.cloned.1.call-start = ((), (), s32[]{:S(2)}) async-start(), calls=%async_computation.4 | async-start | bytes 1966080 | tf_op jit(solution)/shard_map/all_gather | solution.py:144
  374.0 45.3 %copy-start.64 = (pred[4]{0:T(512)(128)(4,1)}, pred[4]{0:T(512)(128)(4,1)S(1)}, u32[]{:S(2)}) copy-start(pred[4]{0:T(512)(128)(4,1)S(1)} %iota_compare_fusion.1) | copy-start | bytes 16
  410.8 8.4 %collective-permute-start.2 = (bf16[2,16,3072]{2,1,0:T(8,128)(2,1)S(1)}, bf16[2,16,3072]{2,1,0:T(8,128)(2,1)S(1)}, u32[]{:S(2)}, u32[]{:S(2)}) collective-permute-start(bf16[2,16,3072]{2,1,0:T(8,128)(2,1)S(1)} %fusion.138), channel_id=1, source_target_pairs={{0,64},{1,65},{2,66},{3,67},{4,68},{5,69},{6,70},{7,71},{8,72},{9,... | collective-permute-start | bytes 589832 | tf_op jit(solution)/shard_map/ppermute | solution.py:15
  429.0 21.9 %copy-start.40 = (bf16[2,8,2,768]{3,1,2,0:T(8,128)(2,1)}, bf16[2,8,2,768]{3,1,2,0:T(8,128)(2,1)S(1)}, u32[]{:S(2)}) copy-start(bf16[2,8,2,768]{3,1,2,0:T(8,128)(2,1)S(1)} %get-tuple-element.68) | copy-start | bytes 147460
  493.2 45.3 %copy-start.44 = (bf16[2,8,3072]{2,1,0:T(8,128)(2,1)S(1)}, bf16[2,8,3072]{2,1,0:T(8,128)(2,1)}, u32[]{:S(2)}) copy-start(bf16[2,8,3072]{2,1,0:T(8,128)(2,1)} %get-tuple-element.53) | copy-start | bytes 294916
  493.3 152.7 %all-gather.24.cloned.1.call-start = ((), (), s32[]{:S(2)}) async-start(), calls=%async_computation.5 | async-start | bytes 1966080 | tf_op jit(solution)/shard_map/all_gather | solution.py:144
  493.3 45.2 %copy-start.66 = (pred[4]{0:T(512)(128)(4,1)}, pred[4]{0:T(512)(128)(4,1)S(1)}, u32[]{:S(2)}) copy-start(pred[4]{0:T(512)(128)(4,1)S(1)} %iota_compare_fusion.5) | copy-start | bytes 16
  530.1 18.1 %copy-start.32 = (bf16[2,16,3072]{2,1,0:T(8,128)(2,1)}, bf16[2,16,3072]{2,1,0:T(8,128)(2,1)S(1)}, u32[]{:S(2)}) copy-start(bf16[2,16,3072]{2,1,0:T(8,128)(2,1)S(1)} %fusion.139) | copy-start | bytes 589828
  530.1 8.4 %collective-permute-start.3 = (bf16[2,16,3072]{2,1,0:T(8,128)(2,1)S(1)}, bf16[2,16,3072]{2,1,0:T(8,128)(2,1)S(1)}, u32[]{:S(2)}, u32[]{:S(2)}) collective-permute-start(bf16[2,16,3072]{2,1,0:T(8,128)(2,1)S(1)} %fusion.139), channel_id=1, source_target_pairs={{0,64},{1,65},{2,66},{3,67},{4,68},{5,69},{6,70},{7,71},{8,72},{9,... | collective-permute-start | bytes 589832 | tf_op jit(solution)/shard_map/ppermute | solution.py:15
  549.9 21.0 %copy-start.42 = (bf16[2,8,2,768]{3,1,2,0:T(8,128)(2,1)}, bf16[2,8,2,768]{3,1,2,0:T(8,128)(2,1)S(1)}, u32[]{:S(2)}) copy-start(bf16[2,8,2,768]{3,1,2,0:T(8,128)(2,1)S(1)} %get-tuple-element.66) | copy-start | bytes 147460
  610.6 37.0 %copy-start.27 = (bf16[2,16,3072]{2,1,0:T(8,128)(2,1)S(1)}, bf16[2,16,3072]{2,1,0:T(8,128)(2,1)}, u32[]{:S(2)}) copy-start(bf16[2,16,3072]{2,1,0:T(8,128)(2,1)} %copy-done.26) | copy-start | bytes 589828
  610.6 37.0 %copy-start.29 = (bf16[2,16,3072]{2,1,0:T(8,128)(2,1)S(1)}, bf16[2,16,3072]{2,1,0:T(8,128)(2,1)}, u32[]{:S(2)}) copy-start(bf16[2,16,3072]{2,1,0:T(8,128)(2,1)} %copy-done.28) | copy-start | bytes 589828
  610.6 37.1 %copy-start.31 = (bf16[2,16,3072]{2,1,0:T(8,128)(2,1)S(1)}, bf16[2,16,3072]{2,1,0:T(8,128)(2,1)}, u32[]{:S(2)}) copy-start(bf16[2,16,3072]{2,1,0:T(8,128)(2,1)} %copy-done.30) | copy-start | bytes 589828
  (48 other events, 170.8 us)
Sparse Core Ops, SparseCore 0:
  10.2 52.0 all-gather.13
  136.4 33.1 all-gather.15
  253.8 35.0 all-gather.17
  374.0 35.0 all-gather.19
  493.4 35.0 all-gather.21
  610.8 35.0 all-gather.23
